TPU v7x, 256 devices: a whole 4x4x8 slice. The times are simulated.
256 devices in a mesh: space: 32 (over z, y), exp: 8 (over x, core).
Axes of the slice: x: 4, y: 4, z: 8, core: 2. Of those that a mesh axis runs over, the one named last changes fastest.
Arguments:
- offsets: float32 [3, 8192, 128], P(None, ('space', 'exp')), may hold values from -1 to 1
- strength: float32 [3, 8192, 128], P(None, ('space', 'exp')), may hold values from -1.3 to 1.3
- leaf_cell: int32 [8192], P(('space', 'exp')), may hold values from 0 to 255, as said below
- leaf_count: int32 [32], P('space'), may hold values from 64 to 256, as said below
- leaf_fill: int32 [8192], P(('space', 'exp')), may hold values from 0 to 128, as said below
- near_list: int32 [18, 8192], P(None, ('space', 'exp')), may hold values from 0 to 8191, as said below
- near_count: int32 [8192], P(('space', 'exp')), may hold values from 0 to 18, as said below
Outputs:
- stream: float32 [3, 8192, 128], P(None, ('space', 'exp'))
Inputs may be any that keep to these rules, and one draw needn't show every extreme that they name: `leaf_cell`: within each segment a permutation of the 256 cells of its slab; live slots hold the occupied cells in ascending order, dead slots the other cells in ascending order. `leaf_count`: two neighbouring segments are full in every draw, and some other segment holds exactly 64 live slots. `leaf_fill`: 0 for dead slots. `near_list`: the first near_count[g] entries of column g are the global slots of the live leaves whose cells differ from g's by at most 1 along every coordinate, g included, in ascending order of the offset (first coordinate slowest); the other entries equal g. `near_count`: 0 for dead slots.
All inputs are finite; a program needn't handle non-finite values.
Results may differ from a plain program's by a relative error of at most 0.0003.
Values sent between devices are 32-bit elements; how exact they have to be, the bound alone decides.
A program may use at most 128 MiB of HBM per device.

v0:
```python
import math

import jax
import jax.numpy as jnp
from jax import lax
from jax.experimental import pallas as pl
from jax.experimental.pallas import tpu as pltpu
from jax.sharding import PartitionSpec as P

NODES = [math.cos((2 * k + 1) * math.pi / 8) for k in range(4)]
SMOOTH = 0.01
SCALE = 1.0 / (4.0 * math.pi)
F32 = jnp.float32
BF16 = jnp.bfloat16
VMEM = pl.BlockSpec(memory_space=pltpu.VMEM)
SMEM = pl.BlockSpec(memory_space=pltpu.SMEM)
ANY = pl.BlockSpec(memory_space=pl.ANY)
BIG = 60 * 1024 * 1024
NN = (((1,), (0,)), ((), ()))
NT = (((1,), (1,)), ((), ()))


def iota(shape, axis):
    return lax.broadcasted_iota(jnp.int32, shape, axis)


def split2(x):
    hi = x.astype(BF16)
    return hi, (x - hi.astype(F32)).astype(BF16)


def split3(x):
    hi = x.astype(BF16).astype(F32)
    rest = x - hi
    mid = rest.astype(BF16).astype(F32)
    return hi, mid, rest - mid


def bdot(a, b, dims=NN):
    return lax.dot_general(a, b, dims, preferred_element_type=F32)


def dot3(a, b, dims=NN):
    ah, al = a if isinstance(a, tuple) else split2(a)
    bh, bl = b if isinstance(b, tuple) else split2(b)
    return bdot(ah, bh, dims) + (bdot(al, bh, dims) + bdot(ah, bl, dims))


def pick_exact(one_hot, x):
    hi = x.astype(BF16)
    rest = x - hi.astype(F32)
    mid = rest.astype(BF16)
    low = (rest - mid.astype(F32)).astype(BF16)
    return bdot(one_hot, hi) + (bdot(one_hot, mid) + bdot(one_hot, low))


def node(k):
    return jnp.where(
        k == 0, NODES[0], jnp.where(k == 1, NODES[1], jnp.where(k == 2, NODES[2], NODES[3]))
    ).astype(F32)


def cheb(u):
    return u, 2.0 * u * u - 1.0, (4.0 * u * u - 3.0) * u


def factors(u):
    t1, t2, t3 = cheb(u)
    out = []
    for t in NODES:
        out.append(0.25 + t1 * (0.5 * t) + t2 * (0.5 * (2 * t * t - 1)) + t3 * (0.5 * (4 * t**3 - 3 * t)))
    return out


def cheb_pair(u, t):
    u1, u2, u3 = cheb(u)
    t1, t2, t3 = cheb(t)
    return 0.25 + 0.5 * (u1 * t1 + u2 * t2 + u3 * t3)


def column(row, count):
    spread = jnp.where(iota((count, count), 0) == iota((count, count), 1), row.astype(F32), 0.0)
    return jnp.sum(spread, axis=1, keepdims=True)


def weights_loop(offs, visit):
    fx, fy, fz = (factors(o) for o in offs)
    for i in range(4):
        for j in range(4):
            fxy = fx[i] * fy[j]
            for k in range(4):
                visit(16 * i + 4 * j + k, fxy * fz[k])


def particles(seg, ex, off_ref, str_ref, cell_ref, count_ref, fill_ref, rec_ref, mul_ref):
    leaf, size = off_ref.shape[1], off_ref.shape[2]
    cell_f = column(cell_ref[...], leaf)
    fill = column(fill_ref[...], leaf)
    cell = cell_f.astype(jnp.int32)
    slot = ex * leaf + iota((leaf, size), 0)
    alive = (slot < count_ref[0]) & (iota((leaf, size), 1).astype(F32) < fill)
    centre = (
        2 * seg + ((cell >> 1) & 1),
        cell >> 2,
        cell & 1,
    )
    offs = [off_ref[a] for a in range(3)]
    charge = []
    for a in range(3):
        pos = (centre[a].astype(F32) + 0.5) + 0.5 * offs[a]
        rec_ref[pl.ds(a, leaf, 6), :] = pos
        q = jnp.where(alive, str_ref[a], 0.0)
        rec_ref[pl.ds(3 + a, leaf, 6), :] = q
        charge.append(q)
    lane = iota((leaf, size), 1)
    acc = [jnp.zeros((leaf, size), F32), jnp.where(lane >= 64, cell_f, 0.0)]

    def visit(a, w):
        for c in range(3):
            total = jnp.sum(charge[c] * w, axis=1, keepdims=True)
            at = a + 64 * (c % 2)
            acc[c // 2] = jnp.where(lane == at, total, acc[c // 2])

    weights_loop(offs, visit)
    mul_ref[0:leaf, :] = acc[0]
    mul_ref[leaf : 2 * leaf, :] = acc[1]


def mesh_at(seg, ex):
    return {"space": seg, "exp": ex}


def remote(src, dst, send, recv, seg, ex):
    return pltpu.make_async_remote_copy(
        src_ref=src, dst_ref=dst, send_sem=send, recv_sem=recv,
        device_id=mesh_at(seg, ex), device_id_type=pl.DeviceIdType.MESH,
    )


def sorted_block(mul_ref, part, guard):
    n_ex, leaf = mul_ref.shape[1], mul_ref.shape[2] // 2
    slots = n_ex * leaf
    par = slots // 8
    m01 = mul_ref[part, :, 0:leaf, :].reshape(slots, 128)
    m2c = mul_ref[part, :, leaf : 2 * leaf, :].reshape(slots, 128)
    cells = jnp.swapaxes(m2c, 0, 1)[64:65, :]
    row = iota((slots, slots), 0)
    wanted = ((row % par) * 8 + row // par).astype(F32)
    one_hot = jnp.where((wanted == cells) & guard, 1.0, 0.0).astype(BF16)
    return pick_exact(one_hot, m01), pick_exact(one_hot, m2c)


def parent_moments(g01, g2):
    par = g01.shape[0] // 8
    total = jnp.zeros((2 * par, 128), F32)
    lane_b = iota((128, 128), 1)
    row_a = iota((128, 128), 0)
    bx, by, bz = (node((lane_b // w) % 4) for w in (16, 4, 1))
    ax, ay, az = (node((row_a // w) % 4) for w in (16, 4, 1))
    sx, sy, sz = ([cheb_pair(bit - 0.5 + 0.5 * a, b) for bit in (0, 1)] for a, b in ((ax, bx), (ay, by), (az, bz)))
    same = (lane_b // 64) == (row_a // 64)
    for h in range(8):
        table = jnp.where(same, sx[(h // 2) % 2] * sy[h // 4] * sz[h % 2], 0.0)
        lhs = jnp.concatenate([g01[h * par : (h + 1) * par], g2[h * par : (h + 1) * par]], axis=0)
        total = total + dot3(lhs, table)
    return total


def store_rows(grid_ref, j, g01, g2):
    par = g01.shape[0] // 8
    for odd in range(2):
        for c in range(3):
            src = g01 if c < 2 else g2
            lo = 64 * (c % 2)
            grid_ref[j * 2 + odd, c, 8 : 8 + par, :] = jnp.concatenate(
                [src[(4 * odd + r) * par : (4 * odd + r + 1) * par, lo : lo + 64] for r in range(4)], axis=1
            )


def m2l_tables(base_ref, near_x_ref):
    lane, row = iota((256, 512), 1), iota((256, 512), 0)
    ux = ((lane // 128) % 2).astype(F32) + 0.5 * node((lane // 16) % 4)
    vx = (row // 128).astype(F32) + 0.5 * node((row // 16) % 4)
    uz = ((lane // 64) % 2).astype(F32) + 0.5 * node(lane % 4)
    vz = ((row // 64) % 2).astype(F32) + 0.5 * node(row % 4)
    base_ref[1] = (uz - vz) * (uz - vz) + SMOOTH
    base_ref[2] = ux - vx
    near_x_ref[1] = ((row // 128) - (lane // 128) % 2).astype(F32)


def m2l_segment(j, par, grid_ref, base_ref, near_x_ref, loc_ref):
    lane1 = iota((1, 512), 1)
    up1 = (lane1 // 256).astype(F32)
    uy = up1 + 0.5 * node((lane1 // 4) % 4)
    vy = 0.5 * node((iota((256, 1), 0) // 4) % 4)
    shift = 2.0 * jnp.asarray(j, jnp.int32).astype(F32) - 2.0
    dx = base_ref[2] - shift
    base_ref[0] = dx * dx + base_ref[1]
    near_x_ref[0] = jnp.where(jnp.abs(near_x_ref[1] + shift) < 1.5, jnp.inf, 0.0)
    for odd in range(2):
        for i in range(3):
            height = 2 * i + odd - 2
            lhs = jnp.concatenate([grid_ref[j * 2 + odd, c, 7 + i : 7 + i + par, :] for c in range(3)], axis=0)
            near_y = jnp.where(jnp.abs(height - up1) < 1.5, jnp.inf, 0.0)
            dy = (uy - height) - vy
            g = lax.rsqrt(dy * dy + base_ref[0] + jnp.minimum(near_x_ref[0], near_y))
            loc_ref[...] += dot3(lhs, g)


def far_tables(seg, ex, per, far_ref):
    wide = per * 64
    lane, row = iota((64, wide), 1), iota((64, wide), 0)
    step = (seg - ex * per - lane // 64).astype(F32)
    dx = 2.0 * step + node(row // 16) - node((lane // 16) % 4)
    dz = node(row % 4) - node(lane % 4)
    far_ref[0] = dx * dx + (dz * dz + SMOOTH)
    far_ref[1] = node((row // 4) % 4) - node((lane // 4) % 4)
    far_ref[2] = jnp.where(jnp.abs(step) < 1.5, jnp.inf, 0.0)


def far_sum(pq_ref, far_ref):
    per = pq_ref.shape[0]
    par = pq_ref.shape[1] // 2
    wide = per * 64
    turn = 7 if (2 * par - 1) % 7 == 0 else 1
    rows = []
    for c in range(3):
        r0, l0 = par * (c // 2), 64 * (c % 2)
        rows.append(jnp.concatenate([pq_ref[q, r0 : r0 + par, l0 : l0 + 64] for q in range(per)], axis=1))
    rows.append(jnp.zeros((128 - 3 * par, wide), F32))
    ph, plo = split2(jnp.swapaxes(jnp.concatenate(rows, axis=0), 0, 1))
    p_to = iota((64, 128), 1) % par

    def some(i, acc):
        high, low = [], []
        for u in range(turn):
            delta = i * turn + u - (par - 1)
            dy = far_ref[1] + 2.0 * delta.astype(F32)
            gap = jnp.where(jnp.abs(delta) <= 1, jnp.inf, 0.0)
            gh, gl = split2(lax.rsqrt(dy * dy + far_ref[0] + jnp.minimum(far_ref[2], gap)))
            high.append(gh)
            low.append(gl)
        gh = jnp.concatenate(high, axis=0)
        got = bdot(gh, ph) + (bdot(jnp.concatenate(low, axis=0), ph) + bdot(gh, plo))
        for u in range(turn):
            delta = i * turn + u - (par - 1)
            moved = pltpu.roll(got[64 * u : 64 * u + 64], (delta + 128) % 128, 1)
            source = p_to - delta
            acc = acc + jnp.where((source >= 0) & (source < par), moved, 0.0)
        return acc

    return lax.fori_loop(0, (2 * par - 1) // turn, some, jnp.zeros((64, 128), F32))


def child_table(table_ref):
    lane, row = iota((64, 512), 1), iota((64, 512), 0)
    table = 1.0
    for bit, w in (((lane // 128) % 2, 16), (lane // 256, 4), ((lane // 64) % 2, 1)):
        table = table * cheb_pair(bit.astype(F32) - 0.5 + 0.5 * node((lane // w) % 4), node((row // w) % 4))
    table_ref[...] = table


def tree_kernel(
    n_seg, n_x, per, off_ref, str_ref, cell_ref, count_ref, fill_ref, win_ref, loc_ref,
    rec_ref, mul_ref, table_ref, mwin_ref, pm_ref, pq_ref, part_ref, share_ref, grid_ref, base_ref, near_x_ref, far_ref,
    send, mrecv, precv, swap_send, swap_recv, share_recv, own_sem,
):
    n_ex = 2 * n_x
    seg, ex = lax.axis_index("space"), lax.axis_index("exp")
    x, core = ex // 2, ex % 2
    prev, after = (seg + n_seg - 1) % n_seg, (seg + 1) % n_seg
    ring = [((x + d) % n_x) * 2 + core for d in range(n_x)]
    mates = [((x + d) % n_x) * 2 + 1 - core for d in range(n_x)]
    order = [1, n_x - 1] + list(range(2, n_x - 1))
    mate = mates[0]
    others = [ring[d] for d in order] + [mates[d] for d in [0] + order]
    there = seg // per
    mine = ex == there
    par = mul_ref.shape[0] // 2 * n_ex // 8
    barrier = pltpu.get_barrier_semaphore()
    sent = []

    def hello(to_seg, to_ex):
        pl.semaphore_signal(barrier, 1, device_id=mesh_at(to_seg, to_ex), device_id_type=pl.DeviceIdType.MESH)

    def not_self(i):
        return jnp.logical_not(mine & (seg % per == i))

    for o in others:
        hello(seg, o)
    hello(prev, ex)
    hello(after, ex)
    for i in range(per):

        @pl.when(not_self(i))
        def _():
            hello(ex * per + i, there)

    particles(seg, ex, off_ref, str_ref, cell_ref, count_ref, fill_ref, rec_ref, mul_ref)
    grid_ref[...] = jnp.zeros(grid_ref.shape, F32)
    loc_ref[...] = jnp.zeros(loc_ref.shape, F32)
    m2l_tables(base_ref, near_x_ref)
    far_tables(seg, ex, per, far_ref)
    child_table(table_ref)
    pl.semaphore_wait(barrier, len(others) + 2 + jnp.where(mine, per - 1, per))

    def push(src, dst, recv, to_seg, to_ex):
        copy = remote(src, dst, send.at[len(sent)], recv, to_seg, to_ex)
        copy.start()
        sent.append(copy)

    def push_m(src, part, who, to_seg, to_ex):
        push(src, mwin_ref.at[part, who], mrecv.at[part, who], to_seg, to_ex)

    def push_p(src, part, who, to_seg, to_ex):
        push(src, win_ref.at[part, who], precv.at[part, who], to_seg, to_ex)

    def got_m(part, who):
        remote(mul_ref, mwin_ref.at[part, who], send.at[0], mrecv.at[part, who], seg, mate).wait_recv()

    def got_p(part, who):
        remote(rec_ref, win_ref.at[part, who], send.at[0], precv.at[part, who], seg, mate).wait_recv()

    for o in others:
        push_m(mul_ref, 1, ex, seg, o)
    push_m(mul_ref, 0, ex, after, ex)
    push_m(mul_ref, 2, ex, prev, ex)
    for d in order:
        push_p(rec_ref, 1, ex, seg, ring[d])
    push_p(rec_ref, 0, ex, after, ex)
    push_p(rec_ref, 2, ex, prev, ex)
    push_p(rec_ref, 1, ex, seg, mate)
    keep = pltpu.make_async_copy(rec_ref, win_ref.at[1, ex], own_sem)
    keep.start()
    mwin_ref[1, ex] = mul_ref[...]
    for d in order:
        got_m(1, ring[d])
        push_m(mwin_ref.at[1, ring[d]], 0, ring[d], after, ex)
        push_m(mwin_ref.at[1, ring[d]], 2, ring[d], prev, ex)
    for d in range(n_x):
        got_m(1, mates[d])
    g01, g2 = sorted_block(mwin_ref, 1, True)
    pm_ref[...] = parent_moments(g01, g2)
    store_rows(grid_ref, 1, g01, g2)

    def pass_on(d):
        got_p(1, ring[d])
        push_p(win_ref.at[1, ring[d]], 0, ring[d], after, ex)
        push_p(win_ref.at[1, ring[d]], 2, ring[d], prev, ex)
        push_p(win_ref.at[1, ring[d]], 1, ring[d], seg, mate)

    def swap(i):
        return remote(pm_ref, pq_ref.at[seg % per], swap_send.at[i], swap_recv.at[seg % per], ex * per + i, there)

    for i in range(per):

        @pl.when(not_self(i))
        def _():
            swap(i).start()

    @pl.when(mine)
    def _():
        pq_ref[seg % per] = pm_ref[...]

    for d in order:
        pass_on(d)
    m2l_segment(1, par, grid_ref, base_ref, near_x_ref, loc_ref)
    for d in [0] + order:
        for part in (0, 2):
            got_m(part, ring[d])
            push_m(mwin_ref.at[part, ring[d]], part, ring[d], seg, mate)

    def pass_mate(d):
        for part in (0, 2):
            got_p(part, ring[d])
            push_p(win_ref.at[part, ring[d]], part, ring[d], seg, mate)

    pass_mate(0)
    for d in range(n_x):
        for part in (0, 2):
            got_m(part, mates[d])
    for part, guard in ((0, seg > 0), (2, seg < n_seg - 1)):
        g01, g2 = sorted_block(mwin_ref, part, guard)
        store_rows(grid_ref, part, g01, g2)

    def sides(i, carry):
        m2l_segment(2 * i, par, grid_ref, base_ref, near_x_ref, loc_ref)
        return carry

    lax.fori_loop(0, 2, sides, 0)
    pass_mate(order[0])
    pass_mate(order[1])
    for i in range(per):

        @pl.when(not_self(i))
        def _():
            remote(pm_ref, pq_ref.at[i], swap_send.at[i], swap_recv.at[i], ex * per + i, there).wait_recv()
            swap(i).wait_send()

    part_ref[...] = far_sum(pq_ref, far_ref)
    for d in order[2:]:
        pass_mate(d)
    for o in others:
        push(part_ref, share_ref.at[ex], share_recv.at[ex], seg, o)
    share_ref[ex] = part_ref[...]
    for d in range(n_x):
        for part in range(3):
            got_p(part, mates[d])
    for o in others:
        remote(part_ref, share_ref.at[o], send.at[0], share_recv.at[o], seg, o).wait_recv()
    parent = share_ref[0]
    for i in range(1, n_ex):
        parent = parent + share_ref[i]
    loc_ref[...] += dot3(jnp.swapaxes(parent, 0, 1)[: 3 * par, :], table_ref[...])
    keep.wait()
    for copy in sent:
        copy.wait_send()


def final_kernel(
    fill_ref, near_ref, many_ref, count_ref, spot_ref, off_ref, cell_ref, win_ref, loc_ref, out_ref,
    box_ref, feat_ref, load_ref, side_ref, sum_ref, sem,
):
    leaf, size = off_ref.shape[1], off_ref.shape[2]
    seg, ex = lax.axis_index("space"), lax.axis_index("exp")
    slots = win_ref.shape[0] // 18
    fetch = pltpu.make_async_copy(win_ref, box_ref.at[0 : slots * 18], sem)
    fetch.start()
    box_ref[slots * 18 :, :] = jnp.zeros((8, size), F32)
    par = slots // 8
    cell = column(cell_ref[...], leaf).astype(jnp.int32)
    chosen = jnp.where((cell >> 3) == iota((leaf, par), 1), 1.0, 0.0).astype(BF16)
    child = cell & 7
    lane = iota((leaf, 128), 1)
    expansion = []
    for c in range(3):
        wide = pick_exact(chosen, loc_ref[c * par : (c + 1) * par, :])
        kept = jnp.zeros((leaf, 128), F32)
        for i in range(4):
            kept = kept + jnp.where(lane // 64 + 2 * i == child, wide[:, 128 * i : 128 * i + 128], 0.0)
        expansion.append(kept + pltpu.roll(kept, 64, 1))
    far = [jnp.zeros((leaf, size), F32) for _ in range(3)]

    def visit(a, w):
        for c in range(3):
            far[c] = far[c] + expansion[c][:, a : a + 1] * w

    weights_loop([off_ref[a] for a in range(3)], visit)
    for c in range(3):
        out_ref[c] = far[c]
    start = (seg - 1) * slots
    row8 = iota((8, size), 0)
    first, second = row8 < 3, (row8 >= 3) & (row8 < 6)
    none = jnp.zeros((8, size), F32)
    count = near_ref.shape[0]
    block = 64
    lane = iota((size, size), 1)
    sum_ref[...] = jnp.zeros(sum_ref.shape, F32)
    fetch.wait()

    def target(t, carry):
        fill = fill_ref[t]
        many = many_ref[t]
        c = spot_ref[t]
        middle = (2 * seg + ((c >> 1) & 1), c >> 2, c & 1)
        mx, my, mz = (jnp.where(row8 == a, m.astype(F32) + 0.5, 0.0) for a, m in enumerate(middle))
        middle = mx + my + mz

        def local(rows):
            near = jnp.where(first, rows - middle, 0.0)
            return near + pltpu.roll(near, 3, 0)

        here = local(box_ref[pl.ds((slots + ex * leaf + t) * 6, 8), :])
        xh, xm, xl = split3(-2.0 * here)
        length = 0.5 * jnp.sum(here * here, axis=0, keepdims=True) + SMOOTH
        nh, nm, nl = split3(length)
        norm = jnp.where(row8 == 3, nh, jnp.where(row8 == 4, nm, nl))
        keep = jnp.where(row8 < 6, 1.0, 0.0)
        cross = jnp.where(first, xh, jnp.where(second, xm, 0.0))
        last = jnp.where(first, xh, jnp.where(second, xl, 0.0))
        tail = jnp.where(first, 1.0, jnp.where(second, norm, 0.0))
        side = jnp.concatenate([cross, cross, last, keep, tail] + [none] * 11, axis=0)
        side_ref[...] = jnp.swapaxes(side, 0, 1).astype(BF16)
        for k in range(count):
            rows = box_ref[pl.ds((near_ref[k, t] - start) * 6, 8), :]
            y = local(rows)
            yh, ym, yl = split3(y)
            sh, sm, sl = split3(y * y)
            feat = [yh, ym, jnp.where(first, yl, yh), jnp.where(first, sh, sm), jnp.where(first, sl, 1.0), none]
            feat_ref[:, size * k : size * k + size] = jnp.concatenate(feat, axis=0).astype(BF16)
            load_ref[k] = rows * jnp.where(k < many, 1.0, 0.0).astype(F32)

        def rows(n, carry):
            at = pl.multiple_of(n * block, block)
            side = side_ref[pl.ds(at, block), 0:48]
            acc = [jnp.zeros((block, size), F32) for _ in range(3)]
            for k in range(0, count, 2):
                g = lax.rsqrt(bdot(side, feat_ref[:, size * k : size * k + 2 * size]))
                for u in range(2):
                    for c in range(3):
                        acc[c] = acc[c] + g[:, size * u : size * u + size] * load_ref[k + u, 3 + c : 4 + c, :]
            for c in range(3):
                sum_ref[c, pl.ds(at, block), :] = acc[c]
            return carry

        lax.fori_loop(0, (fill + block - 1) // block, rows, 0)
        cols = jnp.zeros((size, size), F32)
        for c in range(3):
            cols = jnp.where(lane == c, jnp.sum(sum_ref[c], axis=1, keepdims=True), cols)
        result = jnp.swapaxes(cols, 0, 1)
        live = iota((1, size), 1) < fill
        for c in range(3):
            total = (result[c : c + 1, :] + out_ref[c, pl.ds(t, 1), :]) * SCALE
            out_ref[c, pl.ds(t, 1), :] = jnp.where(live, total, 0.0)
        return carry

    turns = jnp.clip(count_ref[0] - ex * leaf, 0, leaf)
    lax.fori_loop(0, turns, target, 0)

    def blank(t, carry):
        for c in range(3):
            out_ref[c, pl.ds(t, 1), :] = jnp.zeros((1, size), F32)
        return carry

    lax.fori_loop(turns, leaf, blank, 0)


def shape(*dims):
    return jax.ShapeDtypeStruct(dims, F32)


def tree_call(n_seg, n_ex, offsets, strength, cell_row, count, fill_row):
    n_x, per = n_ex // 2, n_seg // n_ex
    leaf, size = offsets.shape[1], offsets.shape[2]
    par = leaf * n_ex // 8
    dma = pltpu.SemaphoreType.DMA
    return pl.pallas_call(
        lambda *refs: tree_kernel(n_seg, n_x, per, *refs),
        out_shape=(shape(3, n_ex, leaf * 6, size), shape(3 * par, 512)),
        in_specs=[VMEM, VMEM, VMEM, SMEM, VMEM],
        out_specs=(ANY, VMEM),
        scratch_shapes=[
            pltpu.VMEM((leaf * 6, size), F32),
            pltpu.VMEM((leaf * 2, size), F32),
            pltpu.VMEM((64, 512), F32),
            pltpu.VMEM((3, n_ex, leaf * 2, size), F32),
            pltpu.VMEM((2 * par, 128), F32),
            pltpu.VMEM((per, 2 * par, 128), F32),
            pltpu.VMEM((64, 128), F32),
            pltpu.VMEM((n_ex, 64, 128), F32),
            pltpu.VMEM((6, 3, par + 16, 256), F32),
            pltpu.VMEM((3, 256, 512), F32),
            pltpu.VMEM((2, 256, 512), F32),
            pltpu.VMEM((3, 64, per * 64), F32),
            dma((14 * n_x + 5,)),
            dma((3, n_ex)),
            dma((3, n_ex)),
            dma((per,)),
            dma((per,)),
            dma((n_ex,)),
            dma,
        ],
        compiler_params=pltpu.CompilerParams(collective_id=0, has_side_effects=True, vmem_limit_bytes=BIG),
    )(offsets, strength, cell_row, count, fill_row)


def final_call(fill, near, many, count, spot, offsets, cell_row, window, loc):
    leaf, size = offsets.shape[1], offsets.shape[2]
    return pl.pallas_call(
        final_kernel,
        out_shape=shape(3, leaf, size),
        in_specs=[SMEM, SMEM, SMEM, SMEM, SMEM, VMEM, VMEM, ANY, VMEM],
        out_specs=VMEM,
        scratch_shapes=[
            pltpu.VMEM((window.shape[0] + 8, size), F32),
            pltpu.VMEM((48, near.shape[0] * size), BF16),
            pltpu.VMEM((near.shape[0], 8, size), F32),
            pltpu.VMEM((size, size), BF16),
            pltpu.VMEM((3, size, size), F32),
            pltpu.SemaphoreType.DMA,
        ],
        compiler_params=pltpu.CompilerParams(vmem_limit_bytes=BIG),
    )(fill, near, many, count, spot, offsets, cell_row, window, loc)


def solution(mesh):
    n_seg, n_ex = mesh.shape["space"], mesh.shape["exp"]

    def body(offsets, strength, leaf_cell, leaf_count, leaf_fill, near_list, near_count):
        leaf, size = offsets.shape[1], offsets.shape[2]
        cell_row = leaf_cell.reshape(1, leaf)
        fill_row = leaf_fill.reshape(1, leaf)
        window, loc = tree_call(n_seg, n_ex, offsets, strength, cell_row, leaf_count, fill_row)
        window = window.reshape(3 * n_ex * leaf * 6, size)
        return final_call(leaf_fill, near_list, near_count, leaf_count, leaf_cell, offsets, cell_row, window, loc)

    in_specs = (
        P(None, ("space", "exp"), None),
        P(None, ("space", "exp"), None),
        P(("space", "exp")),
        P("space"),
        P(("space", "exp")),
        P(None, ("space", "exp")),
        P(("space", "exp")),
    )
    out_specs = P(None, ("space", "exp"), None)
    return jax.shard_map(body, mesh=mesh, in_specs=in_specs, out_specs=out_specs, check_vma=False)
```

profile of v0, /device:TPU:1, one launch (start us, length us, event | category | flops | bytes accessed | tf_op | source)
XLA Modules:
  0.0 77.5 jit_solution(9407722692991975512)
XLA Ops:
  0.7 43.5 %shard_map.73 = (f32[3,8,192,128]{3,2,1,0:T(8,128)}, f32[96,512]{1,0:T(8,128)}) custom-call(f32[3,32,128]{2,1,0:T(8,128)} %off_ref.1, f32[3,32,128]{2,1,0:T(8,128)} %refs_1_.1, s32[1,32]{1,0:T(1,128)} %bitcast.4, s32[1]{0:T(128)S(6)} %copy.8.refs_3_.count_ref, s32[1,32]{1,0:T(1,128)} %bitcast.6), custom_call_target="tpu_custom_call" | custom-call | tf_op jit(solution)/shard_map/pallas_call | solution.py:537
  44.2 33.4 %shard_map.74 = f32[3,32,128]{2,1,0:T(8,128)} custom-call(s32[32]{0:T(128)} %fill_ref.1, s32[18,32]{1,0:T(8,128)} %near_ref.1, s32[32]{0:T(128)} %many_ref.1, s32[1]{0:T(128)S(6)} %copy.8.refs_3_.count_ref, s32[32]{0:T(128)} %spot_ref.1, f32[3,32,128]{2,1,0:T(8,128)} %off_ref.1, s32[1,32]{1,0:T(1,128)} %bitcast.5, f32[4608,128]{1,0:T(8,128)} %bitcast.3, ...), custom_call_target="tpu_custom_call" | custom-call | tf_op jit(solution)/shard_map/pallas_call | solution.py:569
where the time goes:
time: 77.4 us; the launch traced here: 77.5 us
  Pallas kernels  76.9 us (99%)
    pallas_call x1, Pallas kernels, tree_call(): pl.pallas_call(lambda *refs: tree_kernel(n_seg, n_x, per, *refs), out_sha...  43.5 us
    pallas_call x1, Pallas kernels, final_call(): pl.pallas_call(final_kernel, out_shape=shape(3, leaf, size), in_specs=[SM...  33.4 us

commit v1 on v0

--- a/solution.py
+++ b/solution.py
@@ -417,17 +417,100 @@
         copy.wait_send()
 
 
-def final_kernel(
-    fill_ref, near_ref, many_ref, count_ref, spot_ref, off_ref, cell_ref, win_ref, loc_ref, out_ref,
-    box_ref, feat_ref, load_ref, side_ref, sum_ref, sem,
-):
+def near_field(seg, ex, leaf, near_ref, many_ref, spot_ref, box_ref, bufs, cols_ref, near_out_ref):
+    count, size = near_ref.shape[0], 128
+    slots = (box_ref.shape[0] - 8) // 18
+    start = (seg - 1) * slots
+    row8 = iota((8, size), 0)
+    first, second = row8 < 3, (row8 >= 3) & (row8 < 6)
+    none = jnp.zeros((8, size), F32)
+    keep = jnp.where(row8 < 6, 1.0, 0.0)
+    block = 32
+
+    def frame(t):
+        c = spot_ref[t]
+        spot = (2 * seg + ((c >> 1) & 1), c >> 2, c & 1)
+        mx, my, mz = (jnp.where(row8 == a, m.astype(F32) + 0.5, 0.0) for a, m in enumerate(spot))
+        return mx + my + mz
+
+    def local(rows, middle):
+        near = jnp.where(first, rows - middle, 0.0)
+        return near + pltpu.roll(near, 3, 0)
+
+    def target_side(t, middle):
+        here = local(box_ref[pl.ds((slots + ex * leaf + t) * 6, 8), :], middle)
+        xh, xm, xl = split3(-2.0 * here)
+        length = 0.5 * jnp.sum(here * here, axis=0, keepdims=True) + SMOOTH
+        nh, nm, nl = split3(length)
+        norm = jnp.where(row8 == 3, nh, jnp.where(row8 == 4, nm, nl))
+        cross = jnp.where(first, xh, jnp.where(second, xm, 0.0))
+        last = jnp.where(first, xh, jnp.where(second, xl, 0.0))
+        tail = jnp.where(first, 1.0, jnp.where(second, norm, 0.0))
+        side = jnp.concatenate([cross, cross, last, keep, tail] + [none] * 11, axis=0)
+        return jnp.swapaxes(side, 0, 1).astype(BF16)[:, 0:48]
+
+    def pair(t, k0, middle, side, many, buf):
+        r2_ref, load_ref = buf
+        feats = []
+        for k in (k0, k0 + 1):
+            rows = box_ref[pl.ds((near_ref[k, t] - start) * 6, 8), :]
+            y = local(rows, middle)
+            yh, ym, yl = split3(y)
+            sh, sm, sl = split3(y * y)
+            feat = [yh, ym, jnp.where(first, yl, yh), jnp.where(first, sh, sm), jnp.where(first, sl, 1.0), none]
+            feats.append(jnp.concatenate(feat, axis=0).astype(BF16))
+            load_ref[k] = rows * jnp.where(k < many, 1.0, 0.0).astype(F32)
+        r2_ref[:, size * k0 : size * k0 + 2 * size] = bdot(side, jnp.concatenate(feats, axis=1))
+
+    def gather_rows(n, buf):
+        r2_ref, load_ref = buf
+        at = block * n
+        acc = [jnp.zeros((block, size), F32) for _ in range(3)]
+        for k in range(count):
+            g = lax.rsqrt(r2_ref[at : at + block, size * k : size * k + size])
+            for c in range(3):
+                acc[c] = acc[c] + g * load_ref[k, 3 + c : 4 + c, :]
+        lane = iota((block, size), 1)
+        s0, s1, s2 = (jnp.sum(x, axis=1, keepdims=True) for x in acc)
+        cols_ref[at : at + block, :] = jnp.where(lane == 0, s0, jnp.where(lane == 1, s1, s2))
+
+    def store(t):
+        result = jnp.swapaxes(cols_ref[...], 0, 1)
+        for c in range(3):
+            near_out_ref[c, pl.ds(t, 1), :] = result[c : c + 1, :]
+
+    def work(t_next, next_buf, t_now, now_buf):
+        jobs = list(range(size // block)) if now_buf is not None else []
+        steps = count // 2
+        if next_buf is not None:
+            middle = frame(t_next)
+            side = target_side(t_next, middle)
+            many = many_ref[t_next]
+        for p in range(steps):
+            if next_buf is not None:
+                pair(t_next, 2 * p, middle, side, many, next_buf)
+            while jobs and (size // block - len(jobs)) * steps < (p + 1) * (size // block):
+                gather_rows(jobs.pop(0), now_buf)
+        if now_buf is not None:
+            store(t_now)
+
+    def run(turns):
+        work(0, bufs[0], None, None)
+
+        def two(i, carry):
+            t = 2 * i
+            work(t + 1, bufs[1], t, bufs[0])
+            work(jnp.minimum(t + 2, leaf - 1), bufs[0], t + 1, bufs[1])
+            return carry
+
+        lax.fori_loop(0, turns, two, 0)
+
+    return run
+
+
+def leaf_far(cell_ref, off_ref, loc_ref):
     leaf, size = off_ref.shape[1], off_ref.shape[2]
-    seg, ex = lax.axis_index("space"), lax.axis_index("exp")
-    slots = win_ref.shape[0] // 18
-    fetch = pltpu.make_async_copy(win_ref, box_ref.at[0 : slots * 18], sem)
-    fetch.start()
-    box_ref[slots * 18 :, :] = jnp.zeros((8, size), F32)
-    par = slots // 8
+    par = loc_ref.shape[0] // 3
     cell = column(cell_ref[...], leaf).astype(jnp.int32)
     chosen = jnp.where((cell >> 3) == iota((leaf, par), 1), 1.0, 0.0).astype(BF16)
     child = cell & 7
@@ -446,83 +529,28 @@
             far[c] = far[c] + expansion[c][:, a : a + 1] * w
 
     weights_loop([off_ref[a] for a in range(3)], visit)
-    for c in range(3):
-        out_ref[c] = far[c]
-    start = (seg - 1) * slots
-    row8 = iota((8, size), 0)
-    first, second = row8 < 3, (row8 >= 3) & (row8 < 6)
-    none = jnp.zeros((8, size), F32)
-    count = near_ref.shape[0]
-    block = 64
-    lane = iota((size, size), 1)
+    return far
+
+
+def final_kernel(
+    near_ref, many_ref, count_ref, spot_ref, fill_ref, off_ref, cell_ref, win_ref, loc_ref, out_ref,
+    box_ref, r2a_ref, r2b_ref, load_a_ref, load_b_ref, cols_ref, sum_ref, sem,
+):
+    leaf, size = off_ref.shape[1], off_ref.shape[2]
+    seg, ex = lax.axis_index("space"), lax.axis_index("exp")
+    rows = win_ref.shape[0]
+    fetch = pltpu.make_async_copy(win_ref, box_ref.at[0:rows], sem)
+    fetch.start()
+    box_ref[rows:, :] = jnp.zeros((8, size), F32)
     sum_ref[...] = jnp.zeros(sum_ref.shape, F32)
     fetch.wait()
-
-    def target(t, carry):
-        fill = fill_ref[t]
-        many = many_ref[t]
-        c = spot_ref[t]
-        middle = (2 * seg + ((c >> 1) & 1), c >> 2, c & 1)
-        mx, my, mz = (jnp.where(row8 == a, m.astype(F32) + 0.5, 0.0) for a, m in enumerate(middle))
-        middle = mx + my + mz
-
-        def local(rows):
-            near = jnp.where(first, rows - middle, 0.0)
-            return near + pltpu.roll(near, 3, 0)
-
-        here = local(box_ref[pl.ds((slots + ex * leaf + t) * 6, 8), :])
-        xh, xm, xl = split3(-2.0 * here)
-        length = 0.5 * jnp.sum(here * here, axis=0, keepdims=True) + SMOOTH
-        nh, nm, nl = split3(length)
-        norm = jnp.where(row8 == 3, nh, jnp.where(row8 == 4, nm, nl))
-        keep = jnp.where(row8 < 6, 1.0, 0.0)
-        cross = jnp.where(first, xh, jnp.where(second, xm, 0.0))
-        last = jnp.where(first, xh, jnp.where(second, xl, 0.0))
-        tail = jnp.where(first, 1.0, jnp.where(second, norm, 0.0))
-        side = jnp.concatenate([cross, cross, last, keep, tail] + [none] * 11, axis=0)
-        side_ref[...] = jnp.swapaxes(side, 0, 1).astype(BF16)
-        for k in range(count):
-            rows = box_ref[pl.ds((near_ref[k, t] - start) * 6, 8), :]
-            y = local(rows)
-            yh, ym, yl = split3(y)
-            sh, sm, sl = split3(y * y)
-            feat = [yh, ym, jnp.where(first, yl, yh), jnp.where(first, sh, sm), jnp.where(first, sl, 1.0), none]
-            feat_ref[:, size * k : size * k + size] = jnp.concatenate(feat, axis=0).astype(BF16)
-            load_ref[k] = rows * jnp.where(k < many, 1.0, 0.0).astype(F32)
-
-        def rows(n, carry):
-            at = pl.multiple_of(n * block, block)
-            side = side_ref[pl.ds(at, block), 0:48]
-            acc = [jnp.zeros((block, size), F32) for _ in range(3)]
-            for k in range(0, count, 2):
-                g = lax.rsqrt(bdot(side, feat_ref[:, size * k : size * k + 2 * size]))
-                for u in range(2):
-                    for c in range(3):
-                        acc[c] = acc[c] + g[:, size * u : size * u + size] * load_ref[k + u, 3 + c : 4 + c, :]
-            for c in range(3):
-                sum_ref[c, pl.ds(at, block), :] = acc[c]
-            return carry
-
-        lax.fori_loop(0, (fill + block - 1) // block, rows, 0)
-        cols = jnp.zeros((size, size), F32)
-        for c in range(3):
-            cols = jnp.where(lane == c, jnp.sum(sum_ref[c], axis=1, keepdims=True), cols)
-        result = jnp.swapaxes(cols, 0, 1)
-        live = iota((1, size), 1) < fill
-        for c in range(3):
-            total = (result[c : c + 1, :] + out_ref[c, pl.ds(t, 1), :]) * SCALE
-            out_ref[c, pl.ds(t, 1), :] = jnp.where(live, total, 0.0)
-        return carry
-
+    bufs = ((r2a_ref, load_a_ref), (r2b_ref, load_b_ref))
     turns = jnp.clip(count_ref[0] - ex * leaf, 0, leaf)
-    lax.fori_loop(0, turns, target, 0)
-
-    def blank(t, carry):
-        for c in range(3):
-            out_ref[c, pl.ds(t, 1), :] = jnp.zeros((1, size), F32)
-        return carry
-
-    lax.fori_loop(turns, leaf, blank, 0)
+    near_field(seg, ex, leaf, near_ref, many_ref, spot_ref, box_ref, bufs, cols_ref, sum_ref)((turns + 1) // 2)
+    far = leaf_far(cell_ref, off_ref, loc_ref)
+    live = (iota((leaf, size), 1).astype(F32) < column(fill_ref[...], leaf)) & (iota((leaf, size), 0) < turns)
+    for c in range(3):
+        out_ref[c] = jnp.where(live, (far[c] + sum_ref[c]) * SCALE, 0.0)
 
 
 def shape(*dims):
@@ -564,23 +592,28 @@
     )(offsets, strength, cell_row, count, fill_row)
 
 
-def final_call(fill, near, many, count, spot, offsets, cell_row, window, loc):
+def near_scratch(rows, count, leaf, size):
+    return [
+        pltpu.VMEM((rows + 8, size), F32),
+        pltpu.VMEM((size, count * size), F32),
+        pltpu.VMEM((size, count * size), F32),
+        pltpu.VMEM((count, 8, size), F32),
+        pltpu.VMEM((count, 8, size), F32),
+        pltpu.VMEM((size, size), F32),
+        pltpu.VMEM((3, leaf, size), F32),
+    ]
+
+
+def final_call(near, many, count, spot, fill_row, offsets, cell_row, window, loc):
     leaf, size = offsets.shape[1], offsets.shape[2]
     return pl.pallas_call(
         final_kernel,
         out_shape=shape(3, leaf, size),
-        in_specs=[SMEM, SMEM, SMEM, SMEM, SMEM, VMEM, VMEM, ANY, VMEM],
+        in_specs=[SMEM, SMEM, SMEM, SMEM, VMEM, VMEM, VMEM, ANY, VMEM],
         out_specs=VMEM,
-        scratch_shapes=[
-            pltpu.VMEM((window.shape[0] + 8, size), F32),
-            pltpu.VMEM((48, near.shape[0] * size), BF16),
-            pltpu.VMEM((near.shape[0], 8, size), F32),
-            pltpu.VMEM((size, size), BF16),
-            pltpu.VMEM((3, size, size), F32),
-            pltpu.SemaphoreType.DMA,
-        ],
+        scratch_shapes=near_scratch(window.shape[0], near.shape[0], leaf, size) + [pltpu.SemaphoreType.DMA],
         compiler_params=pltpu.CompilerParams(vmem_limit_bytes=BIG),
-    )(fill, near, many, count, spot, offsets, cell_row, window, loc)
+    )(near, many, count, spot, fill_row, offsets, cell_row, window, loc)
 
 
 def solution(mesh):
@@ -592,7 +625,7 @@
         fill_row = leaf_fill.reshape(1, leaf)
         window, loc = tree_call(n_seg, n_ex, offsets, strength, cell_row, leaf_count, fill_row)
         window = window.reshape(3 * n_ex * leaf * 6, size)
-        return final_call(leaf_fill, near_list, near_count, leaf_count, leaf_cell, offsets, cell_row, window, loc)
+        return final_call(near_list, near_count, leaf_count, leaf_cell, fill_row, offsets, cell_row, window, loc)
 
     in_specs = (
         P(None, ("space", "exp"), None),

time: 77.4 us -> 65.4 us (0.84)
  Pallas kernels: 76.9 us -> 64.5 us
    pallas_call x1, Pallas kernels: 33.4 us -> 21 us  [final_call(): pl.pallas_call(final_kernel, out_shape=shape(3, leaf, size), in_specs=[SM...]
where the time goes in v1:
time: 65.4 us; the launch traced here: 65.2 us
  Pallas kernels  64.5 us (99%)
  between operations  0.66 us (1%)
    pallas_call x1, Pallas kernels, tree_call(): pl.pallas_call(lambda *refs: tree_kernel(n_seg, n_x, per, *refs), out_sha...  43.5 us
    pallas_call x1, Pallas kernels, final_call(): pl.pallas_call(final_kernel, out_shape=shape(3, leaf, size), in_specs=[SM...  21 us

profile of v1, /device:TPU:1, one launch (start us, length us, event | category | flops | bytes accessed | tf_op | source)
XLA Modules:
  0.0 65.2 jit_solution(13873782991939195548)
XLA Ops:
  0.7 43.5 %shard_map.73 = (f32[3,8,192,128]{3,2,1,0:T(8,128)}, f32[96,512]{1,0:T(8,128)}) custom-call(f32[3,32,128]{2,1,0:T(8,128)} %off_ref.1, f32[3,32,128]{2,1,0:T(8,128)} %refs_1_.1, s32[1,32]{1,0:T(1,128)} %bitcast.4, s32[1]{0:T(128)S(6)} %copy.8.refs_3_.count_ref, s32[1,32]{1,0:T(1,128)} %bitcast.6), custom_call_target="tpu_custom_call" | custom-call | tf_op jit(solution)/shard_map/pallas_call | solution.py:565
  44.2 21.0 %shard_map.74 = f32[3,32,128]{2,1,0:T(8,128)} custom-call(s32[18,32]{1,0:T(8,128)} %near_ref.1, s32[32]{0:T(128)} %many_ref.1, s32[1]{0:T(128)S(6)} %copy.8.refs_3_.count_ref, s32[32]{0:T(128)} %spot_ref.1, s32[1,32]{1,0:T(1,128)} %bitcast.7, f32[3,32,128]{2,1,0:T(8,128)} %off_ref.1, s32[1,32]{1,0:T(1,128)} %bitcast.5, f32[4608,128]{1,0:T(8,128)} %bitcast.3, ...), custom_call_target="tpu_custom_call" | custom-call | tf_op jit(solution)/shard_map/pallas_call | solution.py:609

commit v2 on v1

--- a/solution.py
+++ b/solution.py
@@ -261,8 +261,9 @@
 
 
 def tree_kernel(
-    n_seg, n_x, per, off_ref, str_ref, cell_ref, count_ref, fill_ref, win_ref, loc_ref,
-    rec_ref, mul_ref, table_ref, mwin_ref, pm_ref, pq_ref, part_ref, share_ref, grid_ref, base_ref, near_x_ref, far_ref,
+    n_seg, n_x, per, off_ref, str_ref, cell_ref, count_ref, fill_ref, near_ref, many_ref, spot_ref, out_ref,
+    loc_ref, rec_ref, mul_ref, table_ref, mwin_ref, pm_ref, pq_ref, part_ref, share_ref, grid_ref, base_ref,
+    near_x_ref, far_ref, box_ref, r2a_ref, r2b_ref, load_a_ref, load_b_ref, cols_ref, sum_ref,
     send, mrecv, precv, swap_send, swap_recv, share_recv, own_sem,
 ):
     n_ex = 2 * n_x
@@ -277,8 +278,12 @@
     there = seg // per
     mine = ex == there
     par = mul_ref.shape[0] // 2 * n_ex // 8
+    leaf, size = off_ref.shape[1], off_ref.shape[2]
     barrier = pltpu.get_barrier_semaphore()
     sent = []
+
+    def box(part, who):
+        return box_ref.at[pl.ds(pl.multiple_of((part * n_ex + who) * (leaf * 6), 8), leaf * 6)]
 
     def hello(to_seg, to_ex):
         pl.semaphore_signal(barrier, 1, device_id=mesh_at(to_seg, to_ex), device_id_type=pl.DeviceIdType.MESH)
@@ -302,6 +307,7 @@
     m2l_tables(base_ref, near_x_ref)
     far_tables(seg, ex, per, far_ref)
     child_table(table_ref)
+    box_ref[18 * n_ex * leaf :, :] = jnp.zeros((8, size), F32)
     pl.semaphore_wait(barrier, len(others) + 2 + jnp.where(mine, per - 1, per))
 
     def push(src, dst, recv, to_seg, to_ex):
@@ -313,13 +319,13 @@
         push(src, mwin_ref.at[part, who], mrecv.at[part, who], to_seg, to_ex)
 
     def push_p(src, part, who, to_seg, to_ex):
-        push(src, win_ref.at[part, who], precv.at[part, who], to_seg, to_ex)
+        push(src, box(part, who), precv.at[part, who], to_seg, to_ex)
 
     def got_m(part, who):
         remote(mul_ref, mwin_ref.at[part, who], send.at[0], mrecv.at[part, who], seg, mate).wait_recv()
 
     def got_p(part, who):
-        remote(rec_ref, win_ref.at[part, who], send.at[0], precv.at[part, who], seg, mate).wait_recv()
+        remote(rec_ref, box(part, who), send.at[0], precv.at[part, who], seg, mate).wait_recv()
 
     for o in others:
         push_m(mul_ref, 1, ex, seg, o)
@@ -330,7 +336,7 @@
     push_p(rec_ref, 0, ex, after, ex)
     push_p(rec_ref, 2, ex, prev, ex)
     push_p(rec_ref, 1, ex, seg, mate)
-    keep = pltpu.make_async_copy(rec_ref, win_ref.at[1, ex], own_sem)
+    keep = pltpu.make_async_copy(rec_ref, box(1, ex), own_sem)
     keep.start()
     mwin_ref[1, ex] = mul_ref[...]
     for d in order:
@@ -345,9 +351,9 @@
 
     def pass_on(d):
         got_p(1, ring[d])
-        push_p(win_ref.at[1, ring[d]], 0, ring[d], after, ex)
-        push_p(win_ref.at[1, ring[d]], 2, ring[d], prev, ex)
-        push_p(win_ref.at[1, ring[d]], 1, ring[d], seg, mate)
+        push_p(box(1, ring[d]), 0, ring[d], after, ex)
+        push_p(box(1, ring[d]), 2, ring[d], prev, ex)
+        push_p(box(1, ring[d]), 1, ring[d], seg, mate)
 
     def swap(i):
         return remote(pm_ref, pq_ref.at[seg % per], swap_send.at[i], swap_recv.at[seg % per], ex * per + i, there)
@@ -373,7 +379,7 @@
     def pass_mate(d):
         for part in (0, 2):
             got_p(part, ring[d])
-            push_p(win_ref.at[part, ring[d]], part, ring[d], seg, mate)
+            push_p(box(part, ring[d]), part, ring[d], seg, mate)
 
     pass_mate(0)
     for d in range(n_x):
@@ -406,20 +412,26 @@
     for d in range(n_x):
         for part in range(3):
             got_p(part, mates[d])
+    keep.wait()
+    bufs = ((r2a_ref, load_a_ref), (r2b_ref, load_b_ref))
+    near_field(seg, ex, leaf, n_ex * leaf, near_ref, many_ref, spot_ref, box_ref, bufs, cols_ref, sum_ref)(leaf // 2)
     for o in others:
         remote(part_ref, share_ref.at[o], send.at[0], share_recv.at[o], seg, o).wait_recv()
     parent = share_ref[0]
     for i in range(1, n_ex):
         parent = parent + share_ref[i]
     loc_ref[...] += dot3(jnp.swapaxes(parent, 0, 1)[: 3 * par, :], table_ref[...])
-    keep.wait()
+    far = leaf_far(cell_ref, off_ref, loc_ref)
+    slot = ex * leaf + iota((leaf, size), 0)
+    live = (iota((leaf, size), 1).astype(F32) < column(fill_ref[...], leaf)) & (slot < count_ref[0])
+    for c in range(3):
+        out_ref[c] = jnp.where(live, (far[c] + sum_ref[c]) * SCALE, 0.0)
     for copy in sent:
         copy.wait_send()
 
 
-def near_field(seg, ex, leaf, near_ref, many_ref, spot_ref, box_ref, bufs, cols_ref, near_out_ref):
+def near_field(seg, ex, leaf, slots, near_ref, many_ref, spot_ref, box_ref, bufs, cols_ref, near_out_ref):
     count, size = near_ref.shape[0], 128
-    slots = (box_ref.shape[0] - 8) // 18
     start = (seg - 1) * slots
     row8 = iota((8, size), 0)
     first, second = row8 < 3, (row8 >= 3) & (row8 < 6)
@@ -453,13 +465,13 @@
         r2_ref, load_ref = buf
         feats = []
         for k in (k0, k0 + 1):
-            rows = box_ref[pl.ds((near_ref[k, t] - start) * 6, 8), :]
+            rows = box_ref[pl.ds(jnp.clip(near_ref[k, t] - start, 0, 3 * slots - 1) * 6, 8), :]
             y = local(rows, middle)
             yh, ym, yl = split3(y)
             sh, sm, sl = split3(y * y)
             feat = [yh, ym, jnp.where(first, yl, yh), jnp.where(first, sh, sm), jnp.where(first, sl, 1.0), none]
             feats.append(jnp.concatenate(feat, axis=0).astype(BF16))
-            load_ref[k] = rows * jnp.where(k < many, 1.0, 0.0).astype(F32)
+            load_ref[k] = rows * jnp.clip(many - k, 0, 1).astype(F32)
         r2_ref[:, size * k0 : size * k0 + 2 * size] = bdot(side, jnp.concatenate(feats, axis=1))
 
     def gather_rows(n, buf):
@@ -500,7 +512,7 @@
         def two(i, carry):
             t = 2 * i
             work(t + 1, bufs[1], t, bufs[0])
-            work(jnp.minimum(t + 2, leaf - 1), bufs[0], t + 1, bufs[1])
+            work((t + 2) % leaf, bufs[0], t + 1, bufs[1])
             return carry
 
         lax.fori_loop(0, turns, two, 0)
@@ -532,42 +544,22 @@
     return far
 
 
-def final_kernel(
-    near_ref, many_ref, count_ref, spot_ref, fill_ref, off_ref, cell_ref, win_ref, loc_ref, out_ref,
-    box_ref, r2a_ref, r2b_ref, load_a_ref, load_b_ref, cols_ref, sum_ref, sem,
-):
-    leaf, size = off_ref.shape[1], off_ref.shape[2]
-    seg, ex = lax.axis_index("space"), lax.axis_index("exp")
-    rows = win_ref.shape[0]
-    fetch = pltpu.make_async_copy(win_ref, box_ref.at[0:rows], sem)
-    fetch.start()
-    box_ref[rows:, :] = jnp.zeros((8, size), F32)
-    sum_ref[...] = jnp.zeros(sum_ref.shape, F32)
-    fetch.wait()
-    bufs = ((r2a_ref, load_a_ref), (r2b_ref, load_b_ref))
-    turns = jnp.clip(count_ref[0] - ex * leaf, 0, leaf)
-    near_field(seg, ex, leaf, near_ref, many_ref, spot_ref, box_ref, bufs, cols_ref, sum_ref)((turns + 1) // 2)
-    far = leaf_far(cell_ref, off_ref, loc_ref)
-    live = (iota((leaf, size), 1).astype(F32) < column(fill_ref[...], leaf)) & (iota((leaf, size), 0) < turns)
-    for c in range(3):
-        out_ref[c] = jnp.where(live, (far[c] + sum_ref[c]) * SCALE, 0.0)
-
-
 def shape(*dims):
     return jax.ShapeDtypeStruct(dims, F32)
 
 
-def tree_call(n_seg, n_ex, offsets, strength, cell_row, count, fill_row):
+def tree_call(n_seg, n_ex, offsets, strength, cell_row, count, fill_row, near, many, spot):
     n_x, per = n_ex // 2, n_seg // n_ex
     leaf, size = offsets.shape[1], offsets.shape[2]
     par = leaf * n_ex // 8
     dma = pltpu.SemaphoreType.DMA
     return pl.pallas_call(
         lambda *refs: tree_kernel(n_seg, n_x, per, *refs),
-        out_shape=(shape(3, n_ex, leaf * 6, size), shape(3 * par, 512)),
-        in_specs=[VMEM, VMEM, VMEM, SMEM, VMEM],
-        out_specs=(ANY, VMEM),
+        out_shape=shape(3, leaf, size),
+        in_specs=[VMEM, VMEM, VMEM, SMEM, VMEM, SMEM, SMEM, SMEM],
+        out_specs=VMEM,
         scratch_shapes=[
+            pltpu.VMEM((3 * par, 512), F32),
             pltpu.VMEM((leaf * 6, size), F32),
             pltpu.VMEM((leaf * 2, size), F32),
             pltpu.VMEM((64, 512), F32),
@@ -580,6 +572,7 @@
             pltpu.VMEM((3, 256, 512), F32),
             pltpu.VMEM((2, 256, 512), F32),
             pltpu.VMEM((3, 64, per * 64), F32),
+            *near_scratch(18 * n_ex * leaf, near.shape[0], leaf, size),
             dma((14 * n_x + 5,)),
             dma((3, n_ex)),
             dma((3, n_ex)),
@@ -589,7 +582,7 @@
             dma,
         ],
         compiler_params=pltpu.CompilerParams(collective_id=0, has_side_effects=True, vmem_limit_bytes=BIG),
-    )(offsets, strength, cell_row, count, fill_row)
+    )(offsets, strength, cell_row, count, fill_row, near, many, spot)
 
 
 def near_scratch(rows, count, leaf, size):
@@ -604,18 +597,6 @@
     ]
 
 
-def final_call(near, many, count, spot, fill_row, offsets, cell_row, window, loc):
-    leaf, size = offsets.shape[1], offsets.shape[2]
-    return pl.pallas_call(
-        final_kernel,
-        out_shape=shape(3, leaf, size),
-        in_specs=[SMEM, SMEM, SMEM, SMEM, VMEM, VMEM, VMEM, ANY, VMEM],
-        out_specs=VMEM,
-        scratch_shapes=near_scratch(window.shape[0], near.shape[0], leaf, size) + [pltpu.SemaphoreType.DMA],
-        compiler_params=pltpu.CompilerParams(vmem_limit_bytes=BIG),
-    )(near, many, count, spot, fill_row, offsets, cell_row, window, loc)
-
-
 def solution(mesh):
     n_seg, n_ex = mesh.shape["space"], mesh.shape["exp"]
 
@@ -623,9 +604,9 @@
         leaf, size = offsets.shape[1], offsets.shape[2]
         cell_row = leaf_cell.reshape(1, leaf)
         fill_row = leaf_fill.reshape(1, leaf)
-        window, loc = tree_call(n_seg, n_ex, offsets, strength, cell_row, leaf_count, fill_row)
-        window = window.reshape(3 * n_ex * leaf * 6, size)
-        return final_call(near_list, near_count, leaf_count, leaf_cell, fill_row, offsets, cell_row, window, loc)
+        return tree_call(
+            n_seg, n_ex, offsets, strength, cell_row, leaf_count, fill_row, near_list, near_count, leaf_cell
+        )
 
     in_specs = (
         P(None, ("space", "exp"), None),

time: 65.4 us -> 61.3 us (0.937)
  Pallas kernels: 64.5 us -> 59 us
  local copies, waits for them, and re-layouts: 0 us -> 1.42 us
    pallas_call x1 -> x0, Pallas kernels: 21 us -> none  [final_call(): pl.pallas_call(final_kernel, out_shape=shape(3, leaf, size), in_specs=[SM...]
    pallas_call x1, Pallas kernels: 43.5 us -> 59 us  [tree_call(): pl.pallas_call(lambda *refs: tree_kernel(n_seg, n_x, per, *refs), out_sha...]
    unnamed x0 -> x1, local copies, waits for them, and re-layouts: none -> 1.42 us
where the time goes in v2:
time: 61.3 us; the launch traced here: 61.1 us
  Pallas kernels  59 us (96%)
  local copies, waits for them, and re-layouts  1.42 us (2%)
  between operations  0.66 us (1%)
    pallas_call x1, Pallas kernels, tree_call(): pl.pallas_call(lambda *refs: tree_kernel(n_seg, n_x, per, *refs), out_sha...  59 us
    unnamed x1, local copies, waits for them, and re-layouts  1.42 us

profile of v2, /device:TPU:1, one launch (start us, length us, event | category | flops | bytes accessed | tf_op | source)
XLA Modules:
  0.0 61.1 jit_solution(9994298951602891966)
XLA Ops:
  0.7 59.0 %shard_map.73 = f32[3,32,128]{2,1,0:T(8,128)} custom-call(f32[3,32,128]{2,1,0:T(8,128)} %refs_0_.1, f32[3,32,128]{2,1,0:T(8,128)} %refs_1_.1, s32[1,32]{1,0:T(1,128)} %bitcast.2, s32[1]{0:T(128)S(6)} %copy.9.refs_3_, s32[1,32]{1,0:T(1,128)} %bitcast.3, s32[18,32]{1,0:T(8,128)} %refs_5_.1, s32[32]{0:T(128)} %refs_6_.1, s32[32]{0:T(128)} %refs_7_.1), custom_call_target="tpu_custom_call" | custom-call | tf_op jit(solution)/shard_map/pallas_call | solution.py:556
  59.6 1.4 %copy.10 = f32[3,32,128]{2,1,0:T(8,128)} copy(f32[3,32,128]{2,1,0:T(8,128)} %shard_map.73) | data formatting | bytes 98304

commit v3 on v2

--- a/solution.py
+++ b/solution.py
@@ -263,7 +263,7 @@
 def tree_kernel(
     n_seg, n_x, per, off_ref, str_ref, cell_ref, count_ref, fill_ref, near_ref, many_ref, spot_ref, out_ref,
     loc_ref, rec_ref, mul_ref, table_ref, mwin_ref, pm_ref, pq_ref, part_ref, share_ref, grid_ref, base_ref,
-    near_x_ref, far_ref, box_ref, r2a_ref, r2b_ref, load_a_ref, load_b_ref, cols_ref, sum_ref,
+    near_x_ref, far_ref, box_ref, r2a_ref, r2b_ref, load_a_ref, load_b_ref, cols_ref, sum_ref, side_ref,
     send, mrecv, precv, swap_send, swap_recv, share_recv, own_sem,
 ):
     n_ex = 2 * n_x
@@ -279,6 +279,7 @@
     mine = ex == there
     par = mul_ref.shape[0] // 2 * n_ex // 8
     leaf, size = off_ref.shape[1], off_ref.shape[2]
+    own_rec = rec_ref.at[0 : leaf * 6]
     barrier = pltpu.get_barrier_semaphore()
     sent = []
 
@@ -307,6 +308,8 @@
     m2l_tables(base_ref, near_x_ref)
     far_tables(seg, ex, per, far_ref)
     child_table(table_ref)
+    rec_ref[leaf * 6 :, :] = jnp.zeros((8, size), F32)
+    target_sides(seg, leaf, spot_ref, rec_ref, side_ref)
     box_ref[18 * n_ex * leaf :, :] = jnp.zeros((8, size), F32)
     pl.semaphore_wait(barrier, len(others) + 2 + jnp.where(mine, per - 1, per))
 
@@ -325,18 +328,18 @@
         remote(mul_ref, mwin_ref.at[part, who], send.at[0], mrecv.at[part, who], seg, mate).wait_recv()
 
     def got_p(part, who):
-        remote(rec_ref, box(part, who), send.at[0], precv.at[part, who], seg, mate).wait_recv()
+        remote(own_rec, box(part, who), send.at[0], precv.at[part, who], seg, mate).wait_recv()
 
     for o in others:
         push_m(mul_ref, 1, ex, seg, o)
     push_m(mul_ref, 0, ex, after, ex)
     push_m(mul_ref, 2, ex, prev, ex)
     for d in order:
-        push_p(rec_ref, 1, ex, seg, ring[d])
-    push_p(rec_ref, 0, ex, after, ex)
-    push_p(rec_ref, 2, ex, prev, ex)
-    push_p(rec_ref, 1, ex, seg, mate)
-    keep = pltpu.make_async_copy(rec_ref, box(1, ex), own_sem)
+        push_p(own_rec, 1, ex, seg, ring[d])
+    push_p(own_rec, 0, ex, after, ex)
+    push_p(own_rec, 2, ex, prev, ex)
+    push_p(own_rec, 1, ex, seg, mate)
+    keep = pltpu.make_async_copy(own_rec, box(1, ex), own_sem)
     keep.start()
     mwin_ref[1, ex] = mul_ref[...]
     for d in order:
@@ -394,8 +397,8 @@
         return carry
 
     lax.fori_loop(0, 2, sides, 0)
-    pass_mate(order[0])
-    pass_mate(order[1])
+    for d in order:
+        pass_mate(d)
     for i in range(per):
 
         @pl.when(not_self(i))
@@ -404,8 +407,6 @@
             swap(i).wait_send()
 
     part_ref[...] = far_sum(pq_ref, far_ref)
-    for d in order[2:]:
-        pass_mate(d)
     for o in others:
         push(part_ref, share_ref.at[ex], share_recv.at[ex], seg, o)
     share_ref[ex] = part_ref[...]
@@ -414,7 +415,7 @@
             got_p(part, mates[d])
     keep.wait()
     bufs = ((r2a_ref, load_a_ref), (r2b_ref, load_b_ref))
-    near_field(seg, ex, leaf, n_ex * leaf, near_ref, many_ref, spot_ref, box_ref, bufs, cols_ref, sum_ref)(leaf // 2)
+    near_field(seg, leaf, n_ex * leaf, near_ref, many_ref, spot_ref, side_ref, box_ref, bufs, cols_ref, sum_ref)(leaf // 2)
     for o in others:
         remote(part_ref, share_ref.at[o], send.at[0], share_recv.at[o], seg, o).wait_recv()
     parent = share_ref[0]
@@ -430,27 +431,26 @@
         copy.wait_send()
 
 
-def near_field(seg, ex, leaf, slots, near_ref, many_ref, spot_ref, box_ref, bufs, cols_ref, near_out_ref):
-    count, size = near_ref.shape[0], 128
-    start = (seg - 1) * slots
-    row8 = iota((8, size), 0)
+def frame(seg, c):
+    row8 = iota((8, 128), 0)
+    spot = (2 * seg + ((c >> 1) & 1), c >> 2, c & 1)
+    mx, my, mz = (jnp.where(row8 == a, m.astype(F32) + 0.5, 0.0) for a, m in enumerate(spot))
+    return mx + my + mz
+
+
+def local(rows, middle):
+    near = jnp.where(iota((8, 128), 0) < 3, rows - middle, 0.0)
+    return near + pltpu.roll(near, 3, 0)
+
+
+def target_sides(seg, leaf, spot_ref, rec_ref, side_ref):
+    row8 = iota((8, 128), 0)
     first, second = row8 < 3, (row8 >= 3) & (row8 < 6)
-    none = jnp.zeros((8, size), F32)
+    none = jnp.zeros((8, 128), F32)
     keep = jnp.where(row8 < 6, 1.0, 0.0)
-    block = 32
-
-    def frame(t):
-        c = spot_ref[t]
-        spot = (2 * seg + ((c >> 1) & 1), c >> 2, c & 1)
-        mx, my, mz = (jnp.where(row8 == a, m.astype(F32) + 0.5, 0.0) for a, m in enumerate(spot))
-        return mx + my + mz
-
-    def local(rows, middle):
-        near = jnp.where(first, rows - middle, 0.0)
-        return near + pltpu.roll(near, 3, 0)
-
-    def target_side(t, middle):
-        here = local(box_ref[pl.ds((slots + ex * leaf + t) * 6, 8), :], middle)
+
+    def one(t):
+        here = local(rec_ref[pl.ds(t * 6, 8), :], frame(seg, spot_ref[t]))
         xh, xm, xl = split3(-2.0 * here)
         length = 0.5 * jnp.sum(here * here, axis=0, keepdims=True) + SMOOTH
         nh, nm, nl = split3(length)
@@ -459,7 +459,23 @@
         last = jnp.where(first, xh, jnp.where(second, xl, 0.0))
         tail = jnp.where(first, 1.0, jnp.where(second, norm, 0.0))
         side = jnp.concatenate([cross, cross, last, keep, tail] + [none] * 11, axis=0)
-        return jnp.swapaxes(side, 0, 1).astype(BF16)[:, 0:48]
+        side_ref[t] = jnp.swapaxes(side, 0, 1).astype(BF16)
+
+    def some(i, carry):
+        for u in range(8):
+            one(8 * i + u)
+        return carry
+
+    lax.fori_loop(0, leaf // 8, some, 0)
+
+
+def near_field(seg, leaf, slots, near_ref, many_ref, spot_ref, side_ref, box_ref, bufs, cols_ref, near_out_ref):
+    count, size = near_ref.shape[0], 128
+    start = (seg - 1) * slots
+    row8 = iota((8, size), 0)
+    first, second = row8 < 3, (row8 >= 3) & (row8 < 6)
+    none = jnp.zeros((8, size), F32)
+    block = 32
 
     def pair(t, k0, middle, side, many, buf):
         r2_ref, load_ref = buf
@@ -495,8 +511,8 @@
         jobs = list(range(size // block)) if now_buf is not None else []
         steps = count // 2
         if next_buf is not None:
-            middle = frame(t_next)
-            side = target_side(t_next, middle)
+            middle = frame(seg, spot_ref[t_next])
+            side = side_ref[t_next, :, 0:48]
             many = many_ref[t_next]
         for p in range(steps):
             if next_buf is not None:
@@ -560,7 +576,7 @@
         out_specs=VMEM,
         scratch_shapes=[
             pltpu.VMEM((3 * par, 512), F32),
-            pltpu.VMEM((leaf * 6, size), F32),
+            pltpu.VMEM((leaf * 6 + 8, size), F32),
             pltpu.VMEM((leaf * 2, size), F32),
             pltpu.VMEM((64, 512), F32),
             pltpu.VMEM((3, n_ex, leaf * 2, size), F32),
@@ -594,6 +610,7 @@
         pltpu.VMEM((count, 8, size), F32),
         pltpu.VMEM((size, size), F32),
         pltpu.VMEM((3, leaf, size), F32),
+        pltpu.VMEM((leaf, size, size), BF16),
     ]
 
 

time: 61.3 us -> 61.4 us (level)
  no operation moved by 1% of the time
where the time goes in v3:
time: 61.4 us; the launch traced here: 61.2 us
  Pallas kernels  59.1 us (96%)
  local copies, waits for them, and re-layouts  1.42 us (2%)
  between operations  0.66 us (1%)
    pallas_call x1, Pallas kernels, tree_call(): pl.pallas_call(lambda *refs: tree_kernel(n_seg, n_x, per, *refs), out_sha...  59.1 us
    unnamed x1, local copies, waits for them, and re-layouts  1.42 us

profile of v3, /device:TPU:1, one launch (start us, length us, event | category | flops | bytes accessed | tf_op | source)
XLA Modules:
  0.0 61.2 jit_solution(5817934613837563543)
XLA Ops:
  0.7 59.1 %shard_map.73 = f32[3,32,128]{2,1,0:T(8,128)} custom-call(f32[3,32,128]{2,1,0:T(8,128)} %refs_0_.1, f32[3,32,128]{2,1,0:T(8,128)} %refs_1_.1, s32[1,32]{1,0:T(1,128)} %bitcast.2, s32[1]{0:T(128)S(6)} %copy.9.refs_3_, s32[1,32]{1,0:T(1,128)} %bitcast.3, s32[18,32]{1,0:T(8,128)} %refs_5_.1, s32[32]{0:T(128)} %refs_6_.1, s32[32]{0:T(128)} %refs_7_.1), custom_call_target="tpu_custom_call" | custom-call | tf_op jit(solution)/shard_map/pallas_call | solution.py:572
  59.7 1.4 %copy.10 = f32[3,32,128]{2,1,0:T(8,128)} copy(f32[3,32,128]{2,1,0:T(8,128)} %shard_map.73) | data formatting | bytes 98304

commit v4 on v3

--- a/solution.py
+++ b/solution.py
@@ -303,13 +303,8 @@
             hello(ex * per + i, there)
 
     particles(seg, ex, off_ref, str_ref, cell_ref, count_ref, fill_ref, rec_ref, mul_ref)
-    grid_ref[...] = jnp.zeros(grid_ref.shape, F32)
-    loc_ref[...] = jnp.zeros(loc_ref.shape, F32)
-    m2l_tables(base_ref, near_x_ref)
     far_tables(seg, ex, per, far_ref)
-    child_table(table_ref)
     rec_ref[leaf * 6 :, :] = jnp.zeros((8, size), F32)
-    target_sides(seg, leaf, spot_ref, rec_ref, side_ref)
     box_ref[18 * n_ex * leaf :, :] = jnp.zeros((8, size), F32)
     pl.semaphore_wait(barrier, len(others) + 2 + jnp.where(mine, per - 1, per))
 
@@ -330,18 +325,23 @@
     def got_p(part, who):
         remote(own_rec, box(part, who), send.at[0], precv.at[part, who], seg, mate).wait_recv()
 
+    push_p(own_rec, 0, ex, after, ex)
+    push_p(own_rec, 2, ex, prev, ex)
     for o in others:
         push_m(mul_ref, 1, ex, seg, o)
     push_m(mul_ref, 0, ex, after, ex)
     push_m(mul_ref, 2, ex, prev, ex)
     for d in order:
         push_p(own_rec, 1, ex, seg, ring[d])
-    push_p(own_rec, 0, ex, after, ex)
-    push_p(own_rec, 2, ex, prev, ex)
     push_p(own_rec, 1, ex, seg, mate)
     keep = pltpu.make_async_copy(own_rec, box(1, ex), own_sem)
     keep.start()
     mwin_ref[1, ex] = mul_ref[...]
+    grid_ref[...] = jnp.zeros(grid_ref.shape, F32)
+    loc_ref[...] = jnp.zeros(loc_ref.shape, F32)
+    m2l_tables(base_ref, near_x_ref)
+    child_table(table_ref)
+    target_sides(seg, leaf, spot_ref, rec_ref, side_ref)
     for d in order:
         got_m(1, ring[d])
         push_m(mwin_ref.at[1, ring[d]], 0, ring[d], after, ex)
@@ -399,23 +399,27 @@
     lax.fori_loop(0, 2, sides, 0)
     for d in order:
         pass_mate(d)
-    for i in range(per):
-
-        @pl.when(not_self(i))
-        def _():
-            remote(pm_ref, pq_ref.at[i], swap_send.at[i], swap_recv.at[i], ex * per + i, there).wait_recv()
-            swap(i).wait_send()
-
-    part_ref[...] = far_sum(pq_ref, far_ref)
-    for o in others:
-        push(part_ref, share_ref.at[ex], share_recv.at[ex], seg, o)
-    share_ref[ex] = part_ref[...]
     for d in range(n_x):
         for part in range(3):
             got_p(part, mates[d])
     keep.wait()
     bufs = ((r2a_ref, load_a_ref), (r2b_ref, load_b_ref))
-    near_field(seg, leaf, n_ex * leaf, near_ref, many_ref, spot_ref, side_ref, box_ref, bufs, cols_ref, sum_ref)(leaf // 2)
+    near = near_field(
+        seg, leaf, n_ex * leaf, near_ref, many_ref, spot_ref, side_ref, box_ref, bufs, cols_ref, sum_ref
+    )
+    near(0, leaf // 4)
+    for i in range(per):
+
+        @pl.when(not_self(i))
+        def _():
+            remote(pm_ref, pq_ref.at[i], swap_send.at[i], swap_recv.at[i], ex * per + i, there).wait_recv()
+            swap(i).wait_send()
+
+    part_ref[...] = far_sum(pq_ref, far_ref)
+    share_ref[ex] = part_ref[...]
+    for o in others:
+        push(part_ref, share_ref.at[ex], share_recv.at[ex], seg, o)
+    near(leaf // 4, leaf // 2)
     for o in others:
         remote(part_ref, share_ref.at[o], send.at[0], share_recv.at[o], seg, o).wait_recv()
     parent = share_ref[0]
@@ -522,8 +526,9 @@
         if now_buf is not None:
             store(t_now)
 
-    def run(turns):
-        work(0, bufs[0], None, None)
+    def run(low, high):
+        if low == 0:
+            work(0, bufs[0], None, None)
 
         def two(i, carry):
             t = 2 * i
@@ -531,7 +536,7 @@
             work((t + 2) % leaf, bufs[0], t + 1, bufs[1])
             return carry
 
-        lax.fori_loop(0, turns, two, 0)
+        lax.fori_loop(low, high, two, 0)
 
     return run
 

time: 61.4 us -> 61.9 us (level)
  no operation moved by 1% of the time
where the time goes in v4:
time: 61.9 us; the launch traced here: 61.6 us
  Pallas kernels  59.6 us (96%)
  local copies, waits for them, and re-layouts  1.42 us (2%)
  between operations  0.66 us (1%)
    pallas_call x1, Pallas kernels, tree_call(): pl.pallas_call(lambda *refs: tree_kernel(n_seg, n_x, per, *refs), out_sha...  59.6 us
    unnamed x1, local copies, waits for them, and re-layouts  1.42 us

profile of v4, /device:TPU:1, one launch (start us, length us, event | category | flops | bytes accessed | tf_op | source)
XLA Modules:
  0.0 61.6 jit_solution(3407853378276149818)
XLA Ops:
  0.7 59.6 %shard_map.73 = f32[3,32,128]{2,1,0:T(8,128)} custom-call(f32[3,32,128]{2,1,0:T(8,128)} %refs_0_.1, f32[3,32,128]{2,1,0:T(8,128)} %refs_1_.1, s32[1,32]{1,0:T(1,128)} %bitcast.2, s32[1]{0:T(128)S(6)} %copy.9.refs_3_, s32[1,32]{1,0:T(1,128)} %bitcast.3, s32[18,32]{1,0:T(8,128)} %refs_5_.1, s32[32]{0:T(128)} %refs_6_.1, s32[32]{0:T(128)} %refs_7_.1), custom_call_target="tpu_custom_call" | custom-call | tf_op jit(solution)/shard_map/pallas_call | solution.py:577
  60.2 1.4 %copy.10 = f32[3,32,128]{2,1,0:T(8,128)} copy(f32[3,32,128]{2,1,0:T(8,128)} %shard_map.73) | data formatting | bytes 98304

commit v5 on v3

--- a/solution.py
+++ b/solution.py
@@ -303,13 +303,8 @@
             hello(ex * per + i, there)
 
     particles(seg, ex, off_ref, str_ref, cell_ref, count_ref, fill_ref, rec_ref, mul_ref)
-    grid_ref[...] = jnp.zeros(grid_ref.shape, F32)
-    loc_ref[...] = jnp.zeros(loc_ref.shape, F32)
-    m2l_tables(base_ref, near_x_ref)
     far_tables(seg, ex, per, far_ref)
-    child_table(table_ref)
     rec_ref[leaf * 6 :, :] = jnp.zeros((8, size), F32)
-    target_sides(seg, leaf, spot_ref, rec_ref, side_ref)
     box_ref[18 * n_ex * leaf :, :] = jnp.zeros((8, size), F32)
     pl.semaphore_wait(barrier, len(others) + 2 + jnp.where(mine, per - 1, per))
 
@@ -342,6 +337,11 @@
     keep = pltpu.make_async_copy(own_rec, box(1, ex), own_sem)
     keep.start()
     mwin_ref[1, ex] = mul_ref[...]
+    grid_ref[...] = jnp.zeros(grid_ref.shape, F32)
+    loc_ref[...] = jnp.zeros(loc_ref.shape, F32)
+    m2l_tables(base_ref, near_x_ref)
+    child_table(table_ref)
+    target_sides(seg, leaf, spot_ref, rec_ref, side_ref)
     for d in order:
         got_m(1, ring[d])
         push_m(mwin_ref.at[1, ring[d]], 0, ring[d], after, ex)

time: 61.4 us -> 61.3 us (level)
  no operation moved by 1% of the time
where the time goes in v5:
time: 61.3 us; the launch traced here: 61.1 us
  Pallas kernels  59 us (96%)
  local copies, waits for them, and re-layouts  1.42 us (2%)
  between operations  0.66 us (1%)
    pallas_call x1, Pallas kernels, tree_call(): pl.pallas_call(lambda *refs: tree_kernel(n_seg, n_x, per, *refs), out_sha...  59 us
    unnamed x1, local copies, waits for them, and re-layouts  1.42 us

profile of v5, /device:TPU:1, one launch (start us, length us, event | category | flops | bytes accessed | tf_op | source)
XLA Modules:
  0.0 61.1 jit_solution(8418739643658766596)
XLA Ops:
  0.7 59.0 %shard_map.73 = f32[3,32,128]{2,1,0:T(8,128)} custom-call(f32[3,32,128]{2,1,0:T(8,128)} %refs_0_.1, f32[3,32,128]{2,1,0:T(8,128)} %refs_1_.1, s32[1,32]{1,0:T(1,128)} %bitcast.2, s32[1]{0:T(128)S(6)} %copy.9.refs_3_, s32[1,32]{1,0:T(1,128)} %bitcast.3, s32[18,32]{1,0:T(8,128)} %refs_5_.1, s32[32]{0:T(128)} %refs_6_.1, s32[32]{0:T(128)} %refs_7_.1), custom_call_target="tpu_custom_call" | custom-call | tf_op jit(solution)/shard_map/pallas_call | solution.py:572
  59.7 1.4 %copy.10 = f32[3,32,128]{2,1,0:T(8,128)} copy(f32[3,32,128]{2,1,0:T(8,128)} %shard_map.73) | data formatting | bytes 98304

commit v6 on v3

--- a/solution.py
+++ b/solution.py
@@ -426,7 +426,7 @@
     slot = ex * leaf + iota((leaf, size), 0)
     live = (iota((leaf, size), 1).astype(F32) < column(fill_ref[...], leaf)) & (slot < count_ref[0])
     for c in range(3):
-        out_ref[c] = jnp.where(live, (far[c] + sum_ref[c]) * SCALE, 0.0)
+        out_ref[c] = jnp.where(live, far[c] + sum_ref[c], 0.0)
     for copy in sent:
         copy.wait_send()
 
@@ -621,9 +621,10 @@
         leaf, size = offsets.shape[1], offsets.shape[2]
         cell_row = leaf_cell.reshape(1, leaf)
         fill_row = leaf_fill.reshape(1, leaf)
-        return tree_call(
+        total = tree_call(
             n_seg, n_ex, offsets, strength, cell_row, leaf_count, fill_row, near_list, near_count, leaf_cell
         )
+        return total * SCALE
 
     in_specs = (
         P(None, ("space", "exp"), None),

time: 61.4 us -> 61.4 us (level)
  other arithmetic: 0 us -> 1.42 us
  local copies, waits for them, and re-layouts: 1.42 us -> 0 us
    mul x0 -> x1, other arithmetic: none -> 1.42 us  [body(): return total * SCALE]
    unnamed x1 -> x0, local copies, waits for them, and re-layouts: 1.42 us -> none
where the time goes in v6:
time: 61.4 us; the launch traced here: 61.2 us
  Pallas kernels  59.1 us (96%)
  other arithmetic  1.42 us (2%)
  between operations  0.66 us (1%)
    pallas_call x1, Pallas kernels, tree_call(): pl.pallas_call(lambda *refs: tree_kernel(n_seg, n_x, per, *refs), out_sha...  59.1 us
    mul x1, other arithmetic, body(): return total * SCALE  1.42 us

profile of v6, /device:TPU:1, one launch (start us, length us, event | category | flops | bytes accessed | tf_op | source)
XLA Modules:
  0.0 61.2 jit_solution(5008011317112223267)
XLA Ops:
  0.7 59.1 %shard_map.73 = f32[3,32,128]{2,1,0:T(8,128)} custom-call(f32[3,32,128]{2,1,0:T(8,128)} %refs_0_.1, f32[3,32,128]{2,1,0:T(8,128)} %refs_1_.1, s32[1,32]{1,0:T(1,128)} %bitcast.2, s32[1]{0:T(128)S(6)} %copy.8.refs_3_, s32[1,32]{1,0:T(1,128)} %bitcast.3, s32[18,32]{1,0:T(8,128)} %refs_5_.1, s32[32]{0:T(128)} %refs_6_.1, s32[32]{0:T(128)} %refs_7_.1), custom_call_target="tpu_custom_call" | custom-call | tf_op jit(solution)/shard_map/pallas_call | solution.py:572
  59.7 1.4 %broadcast_multiply_fusion = f32[3,32,128]{2,1,0:T(8,128)} fusion(f32[3,32,128]{2,1,0:T(8,128)} %shard_map.73), kind=kLoop, calls=%fused_computation | loop fusion | flops 12288 | bytes 98304 | tf_op jit(solution)/shard_map/mul | solution.py:627
